TPU v7x, 32 devices: a whole 2x2x4 slice. The times are simulated.
32 devices in a mesh: groups: 2 (over y), seq: 4 (over z), mp: 2 (over x), section: 2 (over core).
Axes of the slice: x: 2, y: 2, z: 4, core: 2. Of those that a mesh axis runs over, the one named last changes fastest.
Arguments:
- features: bfloat16 [4, 512, 8192], P(('groups', 'section'), 'mp', 'seq'), parts along dimension 0, may hold values from -6 to 6
- alpha: float32 [512], P('mp'), may hold values from 0.5 to 2
- conv_weight: bfloat16 [1024, 32, 16], P('mp'), may hold values from -0.25 to 0.25
- qkv_weight: bfloat16 [1024, 3, 1024], P(None, None, 'mp'), may hold values from -1 to 1
- readout: float32 [1024], P('mp'), may hold values from -4 to 4
- offsets: int32 [4], P(('groups', 'section')), parts along dimension 0, may hold values from 0 to 14479
- pairs: int32 [8, 2], P('groups'), parts along dimension 0, may hold values from 0 to 1
- labels: int32 [8], P('groups'), parts along dimension 0, may hold values from 0 to 1
Outputs:
- grads: bfloat16 [3, 4, 1024, 1024], P(None, ('groups', 'section'), 'seq', 'mp'), parts along dimension 1
- rewards: float32 [4], P('groups'), parts along dimension 0
- loss: float32 [2], P('groups'), parts along dimension 0
There are 2 independent parts, one for each index of `groups`. A program takes and returns all parts, laid end to end along the dimension named above; an argument that names none is the same for every part. Nothing has to cross between parts.
All inputs are finite; a program needn't handle non-finite values.
Results may differ from a plain program's by a relative error of at most 0.017.
Values may be sent and summed in bfloat16 or wider, within the bound.
A program may use at most 64 MiB of HBM per device.

v0:
```python
import math
import jax
import jax.numpy as jnp
from jax import lax
from jax.sharding import PartitionSpec as P

D = 1024
HD = 64
EPS = 1e-06
BASE = 10000.0


def padded_2(block, sides, width):
    for axis, dim in sides:
        count = lax.axis_size(axis)
        forward = [(i, i + 1) for i in range(count - 1)]
        backward = [(target, source) for source, target in forward]
        low = lax.ppermute(
            lax.slice_in_dim(block, block.shape[dim] - width, None, axis=dim), axis, forward
        )
        high = lax.ppermute(lax.slice_in_dim(block, 0, width, axis=dim), axis, backward)
        block = jnp.concatenate([low, block, high], axis=dim)
    return block


def position_table(positions, feature_ids, width):
    pair_ids = (feature_ids // 2).astype(jnp.float32)
    freqs = jnp.exp(pair_ids * (-2.0 * math.log(BASE) / width))
    angle = positions.astype(jnp.float32)[..., None] * freqs
    return jnp.where(feature_ids % 2 == 0, jnp.sin(angle), jnp.cos(angle))


def local(features, alpha, conv_weight, qkv_weight, readout, offsets, pairs, labels):
    f32 = jnp.float32
    bf16 = jnp.bfloat16
    cand, chans, samples = features.shape
    local_width = conv_weight.shape[0]
    per_group = conv_weight.shape[1]
    kern = conv_weight.shape[2]
    stride = kern // 2
    frames_dev = samples // stride
    groups_here = chans // per_group
    heads_here = local_width // HD
    raw = features.astype(f32)
    slope = alpha[None, :, None]
    act = (raw + jnp.sin(slope * raw) ** 2 / slope).astype(bf16)
    padded = padded_2(act, (("seq", 2),), stride // 2)
    blocks = padded.reshape(cand, groups_here, per_group, frames_dev + 1, stride).transpose(
        0, 1, 3, 2, 4
    )
    patches = jnp.concatenate([blocks[:, :, :-1], blocks[:, :, 1:]], axis=-1).reshape(
        cand, groups_here, frames_dev, per_group * kern
    )
    kernel = conv_weight.reshape(groups_here, local_width // groups_here, per_group * kern)
    frames = jnp.einsum("cgfk,gok->cfgo", patches, kernel, preferred_element_type=f32).reshape(
        cand, frames_dev, local_width
    )
    slice_id = lax.axis_index("seq")
    part_id = lax.axis_index("mp")
    positions = (
        offsets[:, None] + slice_id * frames_dev + jnp.arange(frames_dev, dtype=jnp.int32)[None, :]
    )
    feature_ids = part_id * local_width + jnp.arange(local_width, dtype=jnp.int32)
    resid = (frames + position_table(positions, feature_ids, D)).astype(bf16)
    whole = lax.all_gather(resid, "mp", axis=2, tiled=True)
    squares = jnp.mean(jnp.square(whole.astype(f32)), axis=-1)
    projected = jnp.einsum("cfd,dtk->cftk", whole, qkv_weight, preferred_element_type=f32)
    qkv = (projected * lax.rsqrt(squares + EPS)[:, :, None, None]).astype(bf16)
    query = qkv[:, :, 0]
    keys, values = (
        lax.all_gather(qkv[:, :, 1], "seq", axis=1, tiled=True),
        lax.all_gather(qkv[:, :, 2], "seq", axis=1, tiled=True),
    )
    total = keys.shape[1]
    block = min(512, total)
    count_blocks = total // block
    scale = 1.0 / math.sqrt(HD)
    query4 = query.reshape(cand, frames_dev, heads_here, HD)

    def key_slice(source, start, size):
        return lax.dynamic_slice_in_dim(source, start, size, 1).reshape(cand, size, heads_here, HD)

    def scores_for(start, size):
        return (
            jnp.einsum(
                "cfhe,ckhe->chfk", query4, key_slice(keys, start, size), preferred_element_type=f32
            )
            * scale
        )

    def stat_step(carry, index):
        peak_now, mass_now = carry
        score = scores_for(index * block, block)
        fresh = jnp.maximum(peak_now, jnp.max(score, axis=-1))
        mass_now = mass_now * jnp.exp(peak_now - fresh) + jnp.sum(
            jnp.exp(score - fresh[..., None]), axis=-1
        )
        return ((fresh, mass_now), None)

    start_peak = jnp.full((cand, heads_here, frames_dev), -jnp.inf, f32)
    (peak, mass), _ = lax.scan(
        stat_step, (start_peak, jnp.zeros_like(start_peak)), jnp.arange(count_blocks)
    )

    def weights_for(start, size):
        return jnp.exp(scores_for(start, size) - peak[..., None]) / mass[..., None]

    def out_step(running, index):
        start = index * block
        prob = weights_for(start, block).astype(bf16)
        running = running + jnp.einsum(
            "chfk,ckhe->cfhe", prob, key_slice(values, start, block), preferred_element_type=f32
        )
        return (running, None)

    attended4, _ = lax.scan(
        out_step, jnp.zeros((cand, frames_dev, heads_here, HD), f32), jnp.arange(count_blocks)
    )
    attended = attended4.reshape(cand, frames_dev, local_width)
    gate = jax.nn.sigmoid(lax.optimization_barrier(resid).astype(f32))
    section_id = lax.axis_index("section")
    all_cands = cand * lax.axis_size("section")
    owner = (
        jnp.arange(all_cands, dtype=jnp.int32)[None, :]
        == (section_id * cand + jnp.arange(cand, dtype=jnp.int32))[:, None]
    ).astype(f32)
    partial_rewards = jnp.sum(attended * gate * readout, axis=(1, 2)) / math.sqrt(total)
    rewards = lax.psum(jnp.sum(owner * partial_rewards[:, None], axis=0), ("seq", "mp", "section"))
    chosen = (pairs[:, :, None] == jnp.arange(all_cands, dtype=jnp.int32)[None, None, :]).astype(
        f32
    )
    paired = jnp.sum(chosen * rewards[None, None, :], axis=-1)
    margin = paired[:, 0] - paired[:, 1]
    target = labels.astype(f32)
    loss = jnp.sum(jax.nn.softplus(margin) - target * margin)
    coeff = jax.nn.sigmoid(margin) - target
    reward_grad = jnp.sum(coeff[:, None] * (chosen[:, 0] - chosen[:, 1]), axis=0)
    own_grad = jnp.sum(owner * reward_grad[None, :], axis=1)
    upstream = (own_grad[:, None, None] * readout * gate).astype(bf16)
    upstream4 = upstream.reshape(cand, frames_dev, heads_here, HD)
    delta = jnp.sum(upstream4.astype(f32) * attended4, axis=-1).transpose(0, 2, 1)

    def backward_block(start, size):
        prob = weights_for(start, size)
        prob_low = prob.astype(bf16)
        dprob = jnp.einsum(
            "cfhe,ckhe->chfk", upstream4, key_slice(values, start, size), preferred_element_type=f32
        )
        dscore = (prob * (dprob - delta[..., None])).astype(bf16)
        dquery = (
            jnp.einsum(
                "chfk,ckhe->cfhe", dscore, key_slice(keys, start, size), preferred_element_type=f32
            )
            * scale
        )
        dkey = jnp.einsum("chfk,cfhe->kche", dscore, query4, preferred_element_type=f32) * scale
        dvalue = jnp.einsum("chfk,cfhe->kche", prob_low, upstream4, preferred_element_type=f32)
        term = jnp.concatenate(
            [dkey.reshape(size, cand, local_width), dvalue.reshape(size, cand, local_width)],
            axis=-1,
        )
        return (dquery, term)

    zero_query = jnp.zeros((cand, frames_dev, heads_here, HD), f32)

    def grad_step(running, index):
        dquery, term = backward_block(index * block, block)
        return (running + dquery, term.astype(bf16))

    grad_query, stored = lax.scan(grad_step, zero_query, jnp.arange(count_blocks))
    stacked = stored.reshape(total, cand, 2 * local_width)
    summed = lax.psum_scatter(
        stacked.astype(f32).astype(jnp.bfloat16), "seq", scatter_dimension=0, tiled=True
    ).astype(jnp.float32)
    grad_key = summed[:, :, :local_width].transpose(1, 0, 2)
    grad_value = summed[:, :, local_width:].transpose(1, 0, 2)
    grads = jnp.stack(
        [grad_query.reshape(cand, frames_dev, local_width), grad_key, grad_value], axis=0
    ).astype(bf16)
    return (grads, rewards, loss.reshape(1))


def solution(mesh):
    placed = (
        P(("groups", "section"), "mp", "seq"),
        P("mp"),
        P("mp", None, None),
        P(None, None, "mp"),
        P("mp"),
        P(("groups", "section")),
        P("groups", None),
        P("groups"),
    )
    return jax.shard_map(
        local,
        mesh=mesh,
        in_specs=placed,
        out_specs=(P(None, ("groups", "section"), "seq", "mp"), P("groups"), P("groups")),
        check_vma=False,
    )
```

profile of v0, /device:TPU:0, one launch (start us, length us, event | category | flops | bytes accessed | tf_op | source)
XLA Modules:
  0.0 278.7 jit_solution(6267920341593110061)
XLA Ops:
  7.2 8.6 %fusion.25 = bf16[1,256,2048]{2,1,0:T(8,128)(2,1)S(1)} fusion(bf16[1,256,2048]{2,1,0:T(8,128)(2,1)} %param.14, f32[256]{0:T(256)} %param.15), kind=kLoop, calls=%fused_computation.40 | loop fusion | flops 3145728 | bytes 2098176 | tf_op jit(solution)/shard_map/convert_element_type | solution.py:46
  17.0 4.9 %collective-permute-start = (bf16[1,256,4]{2,1,0:T(8,128)(2,1)S(1)}, bf16[1,256,4]{2,1,0:T(8,128)(2,1)S(1)}, u32[]{:S(2)}, u32[]{:S(2)}) collective-permute-start(bf16[1,256,4]{2,1,0:T(8,128)(2,1)S(1)} %get-tuple-element.365), channel_id=1, source_target_pairs={{0,4},{4,8},{8,12},{1,5},{5,9},{9,13},{2,6},{6,10},{10,14},{3,7},{... | collective-permute-start | bytes 6152 | tf_op jit(solution)/shard_map/ppermute | solution.py:18
  24.1 2.4 reshape.438
  28.1 3.5 %concatenate.32 = bf16[1,256,2056]{2,1,0:T(8,128)(2,1)} concatenate(bf16[1,256,4]{2,1,0:T(8,128)(2,1)S(1)} %collective-permute-done, bf16[1,256,2048]{2,1,0:T(8,128)(2,1)} %copy-done.5, bf16[1,256,4]{2,1,0:T(8,128)(2,1)S(1)} %collective-permute-done.1), dimensions={2} | concatenate | bytes 2105344 | tf_op jit(solution)/shard_map/concatenate | solution.py:22
  31.6 2.3 copy.41
  33.9 5.8 %reshape.436 = bf16[1,8,32,257,8]{2,1,4,3,0:T(8,128)(2,1)} reshape(bf16[1,256,2056]{1,2,0:T(8,128)(2,1)} %copy.41) | data formatting | bytes 2105344 | tf_op jit(solution)/shard_map/reshape | solution.py:48
  39.7 6.5 %fusion.53 = (bf16[1,8,256,32,8]{3,1,4,2,0:T(8,128)(2,1)}, bf16[1,8,256,32,8]{3,1,4,2,0:T(8,128)(2,1)}) fusion(bf16[1,8,257,32,8]{3,1,4,2,0:T(8,128)(2,1)} %bitcast.233), kind=kLoop, calls=%fused_computation.102 | loop fusion | bytes 4194304 | tf_op jit(solution)/shard_map/slice | solution.py:51
  46.2 7.7 %copy.42 = bf16[1,8,256,32,8]{2,4,3,1,0:T(8,128)(2,1)} copy(bf16[1,8,256,32,8]{3,1,4,2,0:T(8,128)(2,1)} %get-tuple-element.362) | data formatting | bytes 2097152 | tf_op jit(solution)/shard_map/slice | solution.py:51
  53.9 7.7 %copy.43 = bf16[1,8,256,32,8]{2,4,3,1,0:T(8,128)(2,1)} copy(bf16[1,8,256,32,8]{3,1,4,2,0:T(8,128)(2,1)} %get-tuple-element.363) | data formatting | bytes 2097152 | tf_op jit(solution)/shard_map/slice | solution.py:51
  66.9 3.5 %fusion.31 = bf16[1,256,512]{2,1,0:T(8,128)(2,1)S(1)} fusion(f32[1,256,512]{2,1,0:T(8,128)} %copy.46, f32[512]{0:T(512)S(1)} %fusion.36, f32[256]{0:T(256)S(1)} %add_convert_fusion, pred[512]{0:T(512)(128)(4,1)S(1)} %fusion.33), kind=kLoop, calls=%fused_computation.52 | loop fusion | flops 524288 | bytes 790016 | tf_op jit(solution)/shard_map/convert_element_type | solution.py:64
  71.1 7.3 %all_gather.9 = bf16[1,256,1024]{2,1,0:T(8,128)(2,1)S(1)} all-gather(bf16[1,256,512]{2,1,0:T(8,128)(2,1)S(1)} %fusion.31), channel_id=1, replica_groups=mesh['groups'=2,'seq'=4,'mp'=2,'section'=2] {'mp'}, dimensions={2}, use_global_device_ids=true | all-gather | bytes 786432 | tf_op jit(solution)/shard_map/all_gather | solution.py:65
  82.1 28.3 %all-gather.5.cloned.1.call-done = bf16[1,1024,1,512]{3,1,2,0:T(8,128)(2,1)} async-done(((bf16[1,256,1,512]{3,1,2,0:T(8,128)(2,1)}), bf16[1,1024,1,512]{3,1,2,0:T(8,128)(2,1)}) %all-gather.5.cloned.1.call-update) | async-done | bytes 1048592 | tf_op jit(solution)/shard_map/all_gather | solution.py:71
  110.4 2.3 copy.53
  112.6 16.1 %while.37 = (s32[]{:T(128)}, f32[1,8,256]{2,1,0:T(8,128)S(1)}, f32[1,8,256]{2,1,0:T(8,128)S(1)}, s32[2]{0:T(128)S(1)}, bf16[1,1024,512]{1,2,0:T(8,128)(2,1)}, /*...) while((s32[]{:T(128)}, f32[1,8,256]{2,1,0:T(8,128)S(1)}, ...), condition=%wide.region_4.5_spmd.clone, body=%wide.region_1.4_spmd.clone.sunk | while | flops 139470848 | bytes 10330286 | solution.py:101
  115.0 2.7 bitcast_reduce_fusion.2
  117.7 3.0 %fusion.86 = f32[8,256]{1,0:T(8,128)S(1)} fusion(f32[8,512,256]{2,1,0:T(8,128)} %get-tuple-element.514, f32[8,256]{1,0:T(8,128)S(1)} %bitcast.239), kind=kLoop, calls=%fused_computation.3.clone.1 | loop fusion | flops 3143680 | bytes 4210688 | tf_op jit(solution)/shard_map/while/body/eval_jaxpr/reduce_sum | solution.py:95
  123.1 2.7 bitcast_reduce_fusion.2
  125.8 2.9 %fusion.86 = f32[8,256]{1,0:T(8,128)S(1)} fusion(f32[8,512,256]{2,1,0:T(8,128)} %get-tuple-element.514, f32[8,256]{1,0:T(8,128)S(1)} %bitcast.239), kind=kLoop, calls=%fused_computation.3.clone.1 | loop fusion | flops 3143680 | bytes 4210688 | tf_op jit(solution)/shard_map/while/body/eval_jaxpr/reduce_sum | solution.py:95
  128.7 10.6 %all-gather.7.cloned.1.call-done = bf16[1,1024,1,512]{3,1,2,0:T(8,128)(2,1)} async-done(((bf16[1,256,1,512]{3,1,2,0:T(8,128)(2,1)}), bf16[1,1024,1,512]{3,1,2,0:T(8,128)(2,1)}) %all-gather.7.cloned.1.call-update) | async-done | bytes 1048592 | tf_op jit(solution)/shard_map/all_gather | solution.py:72
  139.4 2.3 copy.54
  141.7 13.9 %while.38 = (s32[]{:T(128)}, f32[1,256,8,64]{1,3,2,0:T(8,128)}, s32[2]{0:T(128)S(1)}, bf16[1,1024,512]{1,2,0:T(8,128)(2,1)}, bf16[1,1024,512]{1,2,0:T(8,128)(2,1...) while((s32[]{:T(128)}, f32[1,256,8,64]{1,3,2,0:T(8,128)}, ...), condition=%wide.region_6.7_spmd.clone, body=%wide.region_5.6_spmd.clone.sunk | while | flops 272891904 | bytes 4473021 | solution.py:116
  142.9 2.3 constant_dynamic-slice_fusion.9
  145.2 3.4 %fusion.90 = f32[1,256,8,64]{1,3,2,0:T(8,128)} fusion(bf16[512,8,64]{0,2,1:T(8,128)(2,1)} %bitcast.236, bf16[512,8,64]{0,2,1:T(8,128)(2,1)} %bitcast.235, f32[8,256]{1,0:T(8,128)S(1)} %bitcast.249, f32[8,256]{1,0:T(8,128)S(1)} %bitcast.245, f32[1,256,8,64]{1,3,2,0:T(8,128)} %get-tuple-element.581, ...), kind=kOutput, calls=%fused_computation.13.clone.1 | convolution fusion | flops 272891904 | bytes 2375681 | tf_op jit(solution)/shard_map/while/body/eval_jaxpr/chfk,ckhe->cfhe/dot_general | solution.py:111
  149.8 2.3 constant_dynamic-slice_fusion.9
  152.0 3.6 %fusion.90 = f32[1,256,8,64]{1,3,2,0:T(8,128)} fusion(bf16[512,8,64]{0,2,1:T(8,128)(2,1)} %bitcast.236, bf16[512,8,64]{0,2,1:T(8,128)(2,1)} %bitcast.235, f32[8,256]{1,0:T(8,128)S(1)} %bitcast.249, f32[8,256]{1,0:T(8,128)S(1)} %bitcast.245, f32[1,256,8,64]{1,3,2,0:T(8,128)} %get-tuple-element.581, ...), kind=kOutput, calls=%fused_computation.13.clone.1 | convolution fusion | flops 272891904 | bytes 2375681 | tf_op jit(solution)/shard_map/while/body/eval_jaxpr/chfk,ckhe->cfhe/dot_general | solution.py:111
  160.3 31.9 %psum.7 = f32[2]{0:T(128)S(1)} all-reduce(f32[2]{0:T(128)S(1)} %compare_select_fusion.2), channel_id=1, replica_groups=mesh['groups'=2,'seq'=4,'mp'=2,'section'=2] {'seq','mp','section'}, use_global_device_ids=true, to_apply=%region_8.9 | all-reduce | flops 2 | bytes 16 | tf_op jit(solution)/shard_map/psum | solution.py:128
  198.3 25.0 %while.39 = (s32[]{:T(128)}, f32[1,256,8,64]{1,3,2,0:T(8,128)}, bf16[2,512,1,1024]{1,3,2,0:T(8,128)(2,1)}, s32[2]{0:T(128)S(1)}, bf16[1,1024,512]{1,2,0:T(8,128)...) while((s32[]{:T(128)}, f32[1,256,8,64]{1,3,2,0:T(8,128)}, ...), condition=%wide.region_14.15_spmd.clone, body=%wide.region_13.14_spmd.clone.sunk | while | flops 681705472 | bytes 39346984 | solution.py:170
  207.7 3.0 %fusion.101 = f32[1,256,8,64]{1,3,2,0:T(8,128)} fusion(bf16[512,8,64]{0,2,1:T(8,128)(2,1)} %bitcast.227, bf16[8,512,256]{2,1,0:T(8,128)(2,1)} %copy-done.1, f32[1,256,8,64]{1,3,2,0:T(8,128)} %get-tuple-element.620, pred[]{:T(512)S(6)} %compare.19), kind=kOutput, calls=%fused_computation.27.clone.1 | convolution fusion | flops 134610944 | bytes 3670017 | tf_op jit(solution)/shard_map/while/body/eval_jaxpr/chfk,ckhe->cfhe/dot_general | solution.py:151
  220.2 3.1 %fusion.101 = f32[1,256,8,64]{1,3,2,0:T(8,128)} fusion(bf16[512,8,64]{0,2,1:T(8,128)(2,1)} %bitcast.227, bf16[8,512,256]{2,1,0:T(8,128)(2,1)} %copy-done.1, f32[1,256,8,64]{1,3,2,0:T(8,128)} %get-tuple-element.620, pred[]{:T(512)S(6)} %compare.19), kind=kOutput, calls=%fused_computation.27.clone.1 | convolution fusion | flops 134610944 | bytes 3670017 | tf_op jit(solution)/shard_map/while/body/eval_jaxpr/chfk,ckhe->cfhe/dot_general | solution.py:151
  223.3 3.3 %copy.58 = bf16[2,1,128,8,512]{4,3,0,2,1:T(8,128)(2,1)} copy(bf16[2,1,128,8,512]{4,3,2,1,0:T(8,128)(2,1)} %bitcast.70) | data formatting | bytes 4194304 | tf_op jit(solution)/shard_map/reshape | solution.py:171
  227.7 40.2 %reduce-scatter.2.cloned.1.call-done = bf16[256,1,1024]{0,2,1:T(8,128)(2,1)} async-done(((bf16[1024,1,1024]{0,2,1:T(8,128)(2,1)}), bf16[256,1,1024]{0,2,1:T(8,128)(2,1)}) %reduce-scatter.2.cloned.1.call-update) | async-done | bytes 524304 | tf_op jit(solution)/shard_map/reduce_scatter | solution.py:172
  269.9 2.3 copy.56
  (100 shorter events, 49.0 us)
Async XLA Ops:
  7.2 71.4 %copy-start = (bf16[1024,3,512]{2,0,1:T(8,128)(2,1)S(1)}, bf16[1024,3,512]{2,0,1:T(8,128)(2,1)}, u32[]{:S(2)}) copy-start(bf16[1024,3,512]{2,0,1:T(8,128)(2,1)} %param.17) | copy-start | bytes 9437188
  7.2 103.2 %all-gather.5.cloned.1.call-start = ((), (), s32[]{:S(2)}) async-start(), calls=%async_computation.2 | async-start | bytes 1310720 | tf_op jit(solution)/shard_map/all_gather | solution.py:71
  15.8 1.0 copy-start.5
  17.0 9.6 %collective-permute-start = (bf16[1,256,4]{2,1,0:T(8,128)(2,1)S(1)}, bf16[1,256,4]{2,1,0:T(8,128)(2,1)S(1)}, u32[]{:S(2)}, u32[]{:S(2)}) collective-permute-start(bf16[1,256,4]{2,1,0:T(8,128)(2,1)S(1)} %get-tuple-element.365), channel_id=1, source_target_pairs={{0,4},{4,8},{8,12},{1,5},{5,9},{9,13},{2,6},{6,10},{10,14},{3,7},{... | collective-permute-start | bytes 6152 | tf_op jit(solution)/shard_map/ppermute | solution.py:18
  21.9 6.2 %collective-permute-start.1 = (bf16[1,256,4]{2,1,0:T(8,128)(2,1)S(1)}, bf16[1,256,4]{2,1,0:T(8,128)(2,1)S(1)}, u32[]{:S(2)}, u32[]{:S(2)}) collective-permute-start(bf16[1,256,4]{2,1,0:T(8,128)(2,1)S(1)} %get-tuple-element.364), channel_id=1, source_target_pairs={{4,0},{8,4},{12,8},{5,1},{9,5},{13,9},{6,2},{10,6},{14,10},{7,3},{... | collective-permute-start | bytes 6152 | tf_op jit(solution)/shard_map/ppermute | solution.py:21
  61.7 1.9 copy-start.6
  70.4 0.7 copy-start.7
  78.6 2.1 copy-start.9
  80.6 58.8 %all-gather.7.cloned.1.call-start = ((), (), s32[]{:S(2)}) async-start(), calls=%async_computation.3 | async-start | bytes 1310720 | tf_op jit(solution)/shard_map/all_gather | solution.py:72
  81.8 186.0 %reduce-scatter.2.cloned.1.call-start = ((), (), s32[]{:S(2)}) async-start(), calls=%async_computation.1 | async-start | bytes 2621440 | tf_op jit(solution)/shard_map/reduce_scatter | solution.py:172
  141.7 16.1 %copy-start.8 = (f32[512]{0:T(512)S(1)}, f32[512]{0:T(512)}, u32[]{:S(2)}) copy-start(f32[512]{0:T(512)} %param.18) | copy-start | bytes 6148
  141.7 50.6 %copy-start.10 = (s32[4]{0:T(128)S(1)}, s32[4]{0:T(128)}, u32[]{:S(2)}) copy-start(s32[4]{0:T(128)} %param.21) | copy-start | bytes 52
  155.6 38.7 %copy-start.3 = (bf16[1,256,8,64]{1,3,2,0:T(8,128)(2,1)}, bf16[1,256,8,64]{1,3,2,0:T(8,128)(2,1)S(1)}, u32[]{:S(2)}) copy-start(bf16[1,256,8,64]{1,3,2,0:T(8,128)(2,1)S(1)} %get-tuple-element.656) | copy-start | bytes 786436
  192.2 6.1 %copy-start.11 = (f32[2]{0:T(128)}, f32[2]{0:T(128)S(1)}, u32[]{:S(2)}) copy-start(f32[2]{0:T(128)S(1)} %psum.7) | copy-start | bytes 28
  200.8 2.2 copy-start.2
  203.0 2.1 copy-start.4
  203.8 1.3 copy-start.1
  213.3 2.2 copy-start.2
  215.5 2.1 copy-start.4
  216.3 1.3 copy-start.1
Sparse Core Ops, SparseCore 0:
  80.7 29.6 all-gather.4
  111.9 27.4 all-gather.6
  226.7 41.0 reduce-scatter.1
where the time goes:
time: 280 us; the launch traced here: 279 us
  waiting for transfers between devices  80.7 us (29%)
  local copies, waits for them, and re-layouts  71.9 us (26%)
  blocking collectives  39.2 us (14%)
  other arithmetic  31.1 us (11%)
  matrix products  29.7 us (11%)
  between operations  15.3 us (5%)
  starting transfers between devices  6.74 us (2%)
  loops' own time  4.08 us (1%)
    reduce_scatter x1, waiting for transfers between devices, local(): lax.psum_scatter(stacked.astype(f32).astype(jnp.bfloat16), 'seq', scatter...  40.2 us
    psum x1, blocking collectives, local(): lax.psum(jnp.sum(owner * partial_rewards[:, None], axis=0), ('seq', 'mp',...  31.9 us
    all_gather x1, waiting for transfers between devices, local(): lax.all_gather(qkv[:, :, 1], 'seq', axis=1, tiled=True)  28.3 us
    slice x2, local copies, waits for them, and re-layouts, local(): blocks[:, :, :-1]  14.2 us
    all_gather x1, waiting for transfers between devices, local(): lax.all_gather(qkv[:, :, 2], 'seq', axis=1, tiled=True)  10.6 us
    dot_general x4, matrix products, scores_for(): jnp.einsum('cfhe,ckhe->chfk', query4, key_slice(keys, start, size), prefe...  9.74 us
    dynamic_slice x6, local copies, waits for them, and re-layouts, key_slice(): lax.dynamic_slice_in_dim(source, start, size, 1)  9.22 us
    unnamed x21, local copies, waits for them, and re-layouts  8.64 us
  transfers between devices with their start and end apart: 5, of which 4 were waited for; matrix products, arithmetic and copies ran while one was open for 8% of the time, Pallas kernels for 0%

commit v1 on v0

--- a/solution.py
+++ b/solution.py
@@ -8,6 +8,44 @@
 HD = 64
 EPS = 1e-06
 BASE = 10000.0
+
+
+def perform_the_sums_all(named_axis, block_in):
+    carry_out, block_next, y_new = (
+        lax.axis_size(named_axis),
+        lax.axis_index(named_axis),
+        block_in.shape[1],
+    )
+    queue = []
+    for num, q in enumerate(block_in.shape):
+        queue.append(q * carry_out if num == 1 else q)
+    prior = lax.dynamic_update_slice_in_dim(
+        jnp.zeros(queue, block_in.dtype), block_in, block_next * y_new, axis=1
+    )
+    w_next = v_now = block_in
+    s = 1
+    while s < carry_out // 2 + 1:
+        by_place = []
+        num = 0
+        while num < carry_out:
+            by_place.append((num, (num + 1) % carry_out))
+            num = num + 1
+        w_next = lax.ppermute(w_next, axis_name=named_axis, perm=by_place)
+        prior = lax.dynamic_update_slice_in_dim(
+            prior, w_next, (block_next - s) % carry_out * y_new, axis=1
+        )
+        if 2 * s < carry_out:
+            views = []
+            num = 0
+            while num < carry_out:
+                views.append((num, (num - 1) % carry_out))
+                num += 1
+            v_now = lax.ppermute(v_now, axis_name=named_axis, perm=views)
+            prior = lax.dynamic_update_slice_in_dim(
+                prior, v_now, (block_next + s) % carry_out * y_new, axis=1
+            )
+        s += 1
+    return prior
 
 
 def padded_2(block, sides, width):
@@ -68,7 +106,7 @@
     qkv = (projected * lax.rsqrt(squares + EPS)[:, :, None, None]).astype(bf16)
     query = qkv[:, :, 0]
     keys, values = (
-        lax.all_gather(qkv[:, :, 1], "seq", axis=1, tiled=True),
+        perform_the_sums_all("seq", qkv[:, :, 1]),
         lax.all_gather(qkv[:, :, 2], "seq", axis=1, tiled=True),
     )
     total = keys.shape[1]

time: 280 us -> 268 us (0.957)
  waiting for transfers between devices: 80.7 us -> 48.3 us
  local copies, waits for them, and re-layouts: 71.9 us -> 84.7 us
  starting transfers between devices: 6.74 us -> 10.7 us
  blocking collectives: 39.2 us -> 42.5 us
    all_gather x1 -> x0, waiting for transfers between devices: 28.3 us -> none  [local(): lax.all_gather(qkv[:, :, 1], 'seq', axis=1, tiled=True)]
    all_gather x1, waiting for transfers between devices: 10.6 us -> 0.02 us  [local(): lax.all_gather(qkv[:, :, 2], 'seq', axis=1, tiled=True)]
    dynamic_update_slice x0 -> x4, local copies, waits for them, and re-layouts: none -> 6.81 us  [the longest x2 3.38 us: perform_the_sums_all(): lax.dynamic_update_slice_in_dim(prior, w_next, (block_next - s) % carry_o...]
    ppermute x0 -> x3, waiting for transfers between devices: none -> 6.36 us  [the longest x2 6.35 us: perform_the_sums_all(): w_next = lax.ppermute(w_next, axis_name=named_axis, perm=by_place)]
    ppermute x0 -> x3, local copies, waits for them, and re-layouts: none -> 5.38 us  [the longest x2 3.6 us: perform_the_sums_all(): w_next = lax.ppermute(w_next, axis_name=named_axis, perm=by_place)]
    ppermute x0 -> x3, starting transfers between devices: none -> 4.18 us  [the longest x1 2.1 us: perform_the_sums_all(): v_now = lax.ppermute(v_now, axis_name=named_axis, perm=views)]
    psum x1, blocking collectives: 31.9 us -> 35.2 us  [local(): lax.psum(jnp.sum(owner * partial_rewards[:, None], axis=0), ('seq', 'mp',...]
    unnamed x21 -> x20, local copies, waits for them, and re-layouts: 8.64 us -> 6.37 us
  transfers between devices with their start and end apart: 5 -> 7, of which waited for: 4 -> 4; matrix products, arithmetic and copies ran while one was open for 8% -> 13% of each run, Pallas kernels for 0% -> 0%
where the time goes in v1:
time: 268 us; the launch traced here: 266 us
  local copies, waits for them, and re-layouts  84.7 us (32%)
  waiting for transfers between devices  48.3 us (18%)
  blocking collectives  42.5 us (16%)
  other arithmetic  31 us (12%)
  matrix products  29.7 us (11%)
  between operations  15.6 us (6%)
  starting transfers between devices  10.7 us (4%)
  loops' own time  4.1 us (2%)
    reduce_scatter x1, waiting for transfers between devices, local(): lax.psum_scatter(stacked.astype(f32).astype(jnp.bfloat16), 'seq', scatter...  40.4 us
    psum x1, blocking collectives, local(): lax.psum(jnp.sum(owner * partial_rewards[:, None], axis=0), ('seq', 'mp',...  35.2 us
    slice x2, local copies, waits for them, and re-layouts, local(): blocks[:, :, :-1]  14.2 us
    dot_general x4, matrix products, scores_for(): jnp.einsum('cfhe,ckhe->chfk', query4, key_slice(keys, start, size), prefe...  9.74 us
    dynamic_slice x6, local copies, waits for them, and re-layouts, key_slice(): lax.dynamic_slice_in_dim(source, start, size, 1)  9.24 us
    convert_element_type x1, other arithmetic, local(): act = (raw + jnp.sin(slope * raw) ** 2 / slope).astype(bf16)  8.61 us
    slice x1, local copies, waits for them, and re-layouts, local(): blocks[:, :, 1:]  7.74 us
    all_gather x1, blocking collectives, local(): whole = lax.all_gather(resid, 'mp', axis=2, tiled=True)  7.28 us
  transfers between devices with their start and end apart: 7, of which 4 were waited for; matrix products, arithmetic and copies ran while one was open for 13% of the time, Pallas kernels for 0%

profile of v1, /device:TPU:0, one launch (start us, length us, event | category | flops | bytes accessed | tf_op | source)
XLA Modules:
  0.0 266.5 jit_solution(2184124154394612736)
XLA Ops:
  7.2 8.6 %fusion.25 = bf16[1,256,2048]{2,1,0:T(8,128)(2,1)S(1)} fusion(bf16[1,256,2048]{2,1,0:T(8,128)(2,1)} %param.14, f32[256]{0:T(256)} %param.15), kind=kLoop, calls=%fused_computation.40 | loop fusion | flops 3145728 | bytes 2098176 | tf_op jit(solution)/shard_map/convert_element_type | solution.py:84
  17.0 4.9 %collective-permute-start = (bf16[1,256,4]{2,1,0:T(8,128)(2,1)S(1)}, bf16[1,256,4]{2,1,0:T(8,128)(2,1)S(1)}, u32[]{:S(2)}, u32[]{:S(2)}) collective-permute-start(bf16[1,256,4]{2,1,0:T(8,128)(2,1)S(1)} %get-tuple-element.353), channel_id=1, source_target_pairs={{0,4},{4,8},{8,12},{1,5},{5,9},{9,13},{2,6},{6,10},{10,14},{3,7},{... | collective-permute-start | bytes 6152 | tf_op jit(solution)/shard_map/ppermute | solution.py:56
  24.1 2.4 reshape.438
  28.1 3.5 %concatenate.32 = bf16[1,256,2056]{2,1,0:T(8,128)(2,1)} concatenate(bf16[1,256,4]{2,1,0:T(8,128)(2,1)S(1)} %collective-permute-done, bf16[1,256,2048]{2,1,0:T(8,128)(2,1)} %copy-done.5, bf16[1,256,4]{2,1,0:T(8,128)(2,1)S(1)} %collective-permute-done.1), dimensions={2} | concatenate | bytes 2105344 | tf_op jit(solution)/shard_map/concatenate | solution.py:60
  31.6 2.3 copy.45
  33.9 5.8 %reshape.436 = bf16[1,8,32,257,8]{2,1,4,3,0:T(8,128)(2,1)} reshape(bf16[1,256,2056]{1,2,0:T(8,128)(2,1)} %copy.45) | data formatting | bytes 2105344 | tf_op jit(solution)/shard_map/reshape | solution.py:86
  39.7 6.5 %fusion.53 = (bf16[1,8,256,32,8]{3,1,4,2,0:T(8,128)(2,1)}, bf16[1,8,256,32,8]{3,1,4,2,0:T(8,128)(2,1)}) fusion(bf16[1,8,257,32,8]{3,1,4,2,0:T(8,128)(2,1)} %bitcast.234), kind=kLoop, calls=%fused_computation.107 | loop fusion | bytes 4194304 | tf_op jit(solution)/shard_map/slice | solution.py:89
  46.2 7.7 %copy.46 = bf16[1,8,256,32,8]{2,4,3,1,0:T(8,128)(2,1)} copy(bf16[1,8,256,32,8]{3,1,4,2,0:T(8,128)(2,1)} %get-tuple-element.350) | data formatting | bytes 2097152 | tf_op jit(solution)/shard_map/slice | solution.py:89
  53.9 7.7 %copy.47 = bf16[1,8,256,32,8]{2,4,3,1,0:T(8,128)(2,1)} copy(bf16[1,8,256,32,8]{3,1,4,2,0:T(8,128)(2,1)} %get-tuple-element.351) | data formatting | bytes 2097152 | tf_op jit(solution)/shard_map/slice | solution.py:89
  66.9 3.5 %fusion.31 = bf16[1,256,512]{2,1,0:T(8,128)(2,1)S(1)} fusion(f32[1,256,512]{2,1,0:T(8,128)} %copy.50, f32[512]{0:T(512)S(1)} %fusion.36, f32[256]{0:T(256)S(1)} %add_convert_fusion, pred[512]{0:T(512)(128)(4,1)S(1)} %fusion.33), kind=kLoop, calls=%fused_computation.52 | loop fusion | flops 524288 | bytes 790016 | tf_op jit(solution)/shard_map/convert_element_type | solution.py:102
  71.1 7.3 %all_gather.6 = bf16[1,256,1024]{2,1,0:T(8,128)(2,1)S(1)} all-gather(bf16[1,256,512]{2,1,0:T(8,128)(2,1)S(1)} %fusion.31), channel_id=1, replica_groups=mesh['groups'=2,'seq'=4,'mp'=2,'section'=2] {'mp'}, dimensions={2}, use_global_device_ids=true | all-gather | bytes 786432 | tf_op jit(solution)/shard_map/all_gather | solution.py:103
  87.6 4.5 %collective-permute-done.2 = bf16[1,256,512]{2,1,0:T(8,128)(2,1)} collective-permute-done((bf16[1,256,512]{2,1,0:T(8,128)(2,1)}, bf16[1,256,512]{2,1,0:T(8,128)(2,1)}, u32[]{:S(2)}, u32[]{:S(2)}) %collective-permute-start.2) | collective-permute-done | bytes 262176 | tf_op jit(solution)/shard_map/ppermute | solution.py:33
  107.4 15.9 %while.37 = (s32[]{:T(128)}, f32[1,8,256]{2,1,0:T(8,128)S(1)}, f32[1,8,256]{2,1,0:T(8,128)S(1)}, s32[2]{0:T(128)S(1)}, bf16[1,1024,512]{1,2,0:T(8,128)(2,1)}, /*...) while((s32[]{:T(128)}, f32[1,8,256]{2,1,0:T(8,128)S(1)}, ...), condition=%wide.region_4.5_spmd.clone, body=%wide.region_1.4_spmd.clone.sunk | while | flops 139470848 | bytes 10330286 | solution.py:139
  109.7 2.7 %bitcast_reduce_fusion.2 = (f32[8,256]{1,0:T(8,128)S(1)}, f32[8,512,256]{2,1,0:T(8,128)}) fusion(bf16[512,8,64]{0,2,1:T(8,128)(2,1)S(1)} %bitcast.229, bf16[1,256,8,64]{1,3,2,0:T(8,128)(2,1)S(1)} %get-tuple-element.551), kind=kOutput, calls=%fused_computation.1.clone.1 | convolution fusion | flops 136312832 | bytes 4988928 | tf_op jit(solution)/shard_map/while/body/eval_jaxpr/cfhe,ckhe->chfk/dot_general | solution.py:123
  112.4 2.9 %fusion.86 = f32[8,256]{1,0:T(8,128)S(1)} fusion(f32[8,512,256]{2,1,0:T(8,128)} %get-tuple-element.502, f32[8,256]{1,0:T(8,128)S(1)} %bitcast.240), kind=kLoop, calls=%fused_computation.3.clone.1 | loop fusion | flops 3143680 | bytes 4210688 | tf_op jit(solution)/shard_map/while/body/eval_jaxpr/reduce_sum | solution.py:133
  117.7 2.7 %bitcast_reduce_fusion.2 = (f32[8,256]{1,0:T(8,128)S(1)}, f32[8,512,256]{2,1,0:T(8,128)}) fusion(bf16[512,8,64]{0,2,1:T(8,128)(2,1)S(1)} %bitcast.229, bf16[1,256,8,64]{1,3,2,0:T(8,128)(2,1)S(1)} %get-tuple-element.551), kind=kOutput, calls=%fused_computation.1.clone.1 | convolution fusion | flops 136312832 | bytes 4988928 | tf_op jit(solution)/shard_map/while/body/eval_jaxpr/cfhe,ckhe->chfk/dot_general | solution.py:123
  120.4 2.9 %fusion.86 = f32[8,256]{1,0:T(8,128)S(1)} fusion(f32[8,512,256]{2,1,0:T(8,128)} %get-tuple-element.502, f32[8,256]{1,0:T(8,128)S(1)} %bitcast.240), kind=kLoop, calls=%fused_computation.3.clone.1 | loop fusion | flops 3143680 | bytes 4210688 | tf_op jit(solution)/shard_map/while/body/eval_jaxpr/reduce_sum | solution.py:133
  123.3 2.3 copy.59
  125.6 14.0 %while.38 = (s32[]{:T(128)}, f32[1,256,8,64]{1,3,2,0:T(8,128)}, s32[2]{0:T(128)S(1)}, bf16[1,1024,512]{1,2,0:T(8,128)(2,1)}, bf16[1,1024,512]{1,2,0:T(8,128)(2,1...) while((s32[]{:T(128)}, f32[1,256,8,64]{1,3,2,0:T(8,128)}, ...), condition=%wide.region_6.7_spmd.clone, body=%wide.region_5.6_spmd.clone.sunk | while | flops 272891904 | bytes 4473021 | solution.py:154
  126.9 2.3 constant_dynamic-slice_fusion.9
  129.1 3.4 %fusion.90 = f32[1,256,8,64]{1,3,2,0:T(8,128)} fusion(bf16[512,8,64]{0,2,1:T(8,128)(2,1)} %bitcast.237, bf16[512,8,64]{0,2,1:T(8,128)(2,1)} %bitcast.236, f32[8,256]{1,0:T(8,128)S(1)} %bitcast.249, f32[8,256]{1,0:T(8,128)S(1)} %bitcast.245, f32[1,256,8,64]{1,3,2,0:T(8,128)} %get-tuple-element.569, ...), kind=kOutput, calls=%fused_computation.13.clone.1 | convolution fusion | flops 272891904 | bytes 2375681 | tf_op jit(solution)/shard_map/while/body/eval_jaxpr/chfk,ckhe->cfhe/dot_general | solution.py:149
  133.8 2.3 constant_dynamic-slice_fusion.9
  136.0 3.6 %fusion.90 = f32[1,256,8,64]{1,3,2,0:T(8,128)} fusion(bf16[512,8,64]{0,2,1:T(8,128)(2,1)} %bitcast.237, bf16[512,8,64]{0,2,1:T(8,128)(2,1)} %bitcast.236, f32[8,256]{1,0:T(8,128)S(1)} %bitcast.249, f32[8,256]{1,0:T(8,128)S(1)} %bitcast.245, f32[1,256,8,64]{1,3,2,0:T(8,128)} %get-tuple-element.569, ...), kind=kOutput, calls=%fused_computation.13.clone.1 | convolution fusion | flops 272891904 | bytes 2375681 | tf_op jit(solution)/shard_map/while/body/eval_jaxpr/chfk,ckhe->cfhe/dot_general | solution.py:149
  144.2 35.2 %psum.7 = f32[2]{0:T(128)S(1)} all-reduce(f32[2]{0:T(128)S(1)} %compare_select_fusion.2), channel_id=1, replica_groups=mesh['groups'=2,'seq'=4,'mp'=2,'section'=2] {'seq','mp','section'}, use_global_device_ids=true, to_apply=%region_8.9 | all-reduce | flops 2 | bytes 16 | tf_op jit(solution)/shard_map/psum | solution.py:166
  185.6 25.0 %while.39 = (s32[]{:T(128)}, f32[1,256,8,64]{1,3,2,0:T(8,128)}, bf16[2,512,1,1024]{1,3,2,0:T(8,128)(2,1)}, s32[2]{0:T(128)S(1)}, bf16[1,1024,512]{1,2,0:T(8,128)...) while((s32[]{:T(128)}, f32[1,256,8,64]{1,3,2,0:T(8,128)}, ...), condition=%wide.region_14.15_spmd.clone, body=%wide.region_13.14_spmd.clone.sunk | while | flops 681705472 | bytes 39346984 | solution.py:208
  188.1 2.2 exponential_divide_fusion.2
  195.0 3.0 %fusion.101 = f32[1,256,8,64]{1,3,2,0:T(8,128)} fusion(bf16[512,8,64]{0,2,1:T(8,128)(2,1)} %bitcast.228, bf16[8,512,256]{2,1,0:T(8,128)(2,1)} %copy-done.1, f32[1,256,8,64]{1,3,2,0:T(8,128)} %get-tuple-element.608, pred[]{:T(512)S(6)} %compare.22), kind=kOutput, calls=%fused_computation.27.clone.1 | convolution fusion | flops 134610944 | bytes 3670017 | tf_op jit(solution)/shard_map/while/body/eval_jaxpr/chfk,ckhe->cfhe/dot_general | solution.py:189
  200.6 2.2 exponential_divide_fusion.2
  207.5 3.1 %fusion.101 = f32[1,256,8,64]{1,3,2,0:T(8,128)} fusion(bf16[512,8,64]{0,2,1:T(8,128)(2,1)} %bitcast.228, bf16[8,512,256]{2,1,0:T(8,128)(2,1)} %copy-done.1, f32[1,256,8,64]{1,3,2,0:T(8,128)} %get-tuple-element.608, pred[]{:T(512)S(6)} %compare.22), kind=kOutput, calls=%fused_computation.27.clone.1 | convolution fusion | flops 134610944 | bytes 3670017 | tf_op jit(solution)/shard_map/while/body/eval_jaxpr/chfk,ckhe->cfhe/dot_general | solution.py:189
  210.6 3.3 %copy.63 = bf16[2,1,128,8,512]{4,3,0,2,1:T(8,128)(2,1)} copy(bf16[2,1,128,8,512]{4,3,2,1,0:T(8,128)(2,1)} %bitcast.70) | data formatting | bytes 4194304 | tf_op jit(solution)/shard_map/reshape | solution.py:209
  214.9 40.4 %reduce-scatter.2.cloned.1.call-done = bf16[256,1,1024]{0,2,1:T(8,128)(2,1)} async-done(((bf16[1024,1,1024]{0,2,1:T(8,128)(2,1)}), bf16[256,1,1024]{0,2,1:T(8,128)(2,1)}) %reduce-scatter.2.cloned.1.call-update) | async-done | bytes 524304 | tf_op jit(solution)/shard_map/reduce_scatter | solution.py:210
  257.3 2.3 copy.61
  (111 shorter events, 65.5 us)
Async XLA Ops:
  7.2 71.4 %copy-start = (bf16[1024,3,512]{2,0,1:T(8,128)(2,1)S(1)}, bf16[1024,3,512]{2,0,1:T(8,128)(2,1)}, u32[]{:S(2)}) copy-start(bf16[1024,3,512]{2,0,1:T(8,128)(2,1)} %param.17) | copy-start | bytes 9437188
  7.2 116.1 %all-gather.3.cloned.1.call-start = ((), (), s32[]{:S(2)}) async-start(), calls=%async_computation.2 | async-start | bytes 1310720 | tf_op jit(solution)/shard_map/all_gather | solution.py:110
  15.8 1.0 copy-start.5
  17.0 9.6 %collective-permute-start = (bf16[1,256,4]{2,1,0:T(8,128)(2,1)S(1)}, bf16[1,256,4]{2,1,0:T(8,128)(2,1)S(1)}, u32[]{:S(2)}, u32[]{:S(2)}) collective-permute-start(bf16[1,256,4]{2,1,0:T(8,128)(2,1)S(1)} %get-tuple-element.353), channel_id=1, source_target_pairs={{0,4},{4,8},{8,12},{1,5},{5,9},{9,13},{2,6},{6,10},{10,14},{3,7},{... | collective-permute-start | bytes 6152 | tf_op jit(solution)/shard_map/ppermute | solution.py:56
  21.9 6.2 %collective-permute-start.1 = (bf16[1,256,4]{2,1,0:T(8,128)(2,1)S(1)}, bf16[1,256,4]{2,1,0:T(8,128)(2,1)S(1)}, u32[]{:S(2)}, u32[]{:S(2)}) collective-permute-start(bf16[1,256,4]{2,1,0:T(8,128)(2,1)S(1)} %get-tuple-element.352), channel_id=1, source_target_pairs={{4,0},{8,4},{12,8},{5,1},{9,5},{13,9},{6,2},{10,6},{14,10},{7,3},{... | collective-permute-start | bytes 6152 | tf_op jit(solution)/shard_map/ppermute | solution.py:59
  61.7 1.9 copy-start.6
  70.4 0.7 copy-start.7
  78.6 6.0 %copy-start.9 = (s32[4,2]{0,1:T(2,128)S(1)}, s32[4,2]{0,1:T(2,128)}, u32[]{:S(2)}) copy-start(s32[4,2]{0,1:T(2,128)} %param.20) | copy-start | bytes 100
  80.5 11.6 %collective-permute-start.2 = (bf16[1,256,512]{2,1,0:T(8,128)(2,1)}, bf16[1,256,512]{2,1,0:T(8,128)(2,1)}, u32[]{:S(2)}, u32[]{:S(2)}) collective-permute-start(bf16[1,256,512]{2,1,0:T(8,128)(2,1)} %get-tuple-element.356), channel_id=1, source_target_pairs={{0,4},{4,8},{8,12},{12,0},{1,5},{5,9},{9,13},{13,1},{2,6},{6,10},{... | collective-permute-start | bytes 786440 | tf_op jit(solution)/shard_map/ppermute | solution.py:33
  82.5 14.3 %collective-permute-start.3 = (bf16[1,256,512]{2,1,0:T(8,128)(2,1)}, bf16[1,256,512]{2,1,0:T(8,128)(2,1)}, u32[]{:S(2)}, u32[]{:S(2)}) collective-permute-start(bf16[1,256,512]{2,1,0:T(8,128)(2,1)} %get-tuple-element.356), channel_id=1, source_target_pairs={{0,12},{4,0},{8,4},{12,8},{1,13},{5,1},{9,5},{13,9},{2,14},{6,2},{... | collective-permute-start | bytes 786440 | tf_op jit(solution)/shard_map/ppermute | solution.py:43
  87.6 167.7 %reduce-scatter.2.cloned.1.call-start = ((), (), s32[]{:S(2)}) async-start(), calls=%async_computation.1 | async-start | bytes 2621440 | tf_op jit(solution)/shard_map/reduce_scatter | solution.py:210
  92.1 11.8 %collective-permute-start.4 = (bf16[1,256,512]{2,1,0:T(8,128)(2,1)}, bf16[1,256,512]{2,1,0:T(8,128)(2,1)}, u32[]{:S(2)}, u32[]{:S(2)}) collective-permute-start(bf16[1,256,512]{2,1,0:T(8,128)(2,1)} %collective-permute-done.2), channel_id=1, source_target_pairs={{0,4},{4,8},{8,12},{12,0},{1,5},{5,9},{9,13},{13,1},{2,6},{6,10},{... | collective-permute-start | bytes 786440 | tf_op jit(solution)/shard_map/ppermute | solution.py:33
  125.6 16.1 %copy-start.8 = (f32[512]{0:T(512)S(1)}, f32[512]{0:T(512)}, u32[]{:S(2)}) copy-start(f32[512]{0:T(512)} %param.18) | copy-start | bytes 6148
  125.6 53.9 %copy-start.10 = (s32[4]{0:T(128)S(1)}, s32[4]{0:T(128)}, u32[]{:S(2)}) copy-start(s32[4]{0:T(128)} %param.21) | copy-start | bytes 52
  139.6 42.0 %copy-start.3 = (bf16[1,256,8,64]{1,3,2,0:T(8,128)(2,1)}, bf16[1,256,8,64]{1,3,2,0:T(8,128)(2,1)S(1)}, u32[]{:S(2)}) copy-start(bf16[1,256,8,64]{1,3,2,0:T(8,128)(2,1)S(1)} %get-tuple-element.641) | copy-start | bytes 786436
  179.5 6.1 %copy-start.11 = (f32[2]{0:T(128)}, f32[2]{0:T(128)S(1)}, u32[]{:S(2)}) copy-start(f32[2]{0:T(128)S(1)} %psum.7) | copy-start | bytes 28
  188.1 2.2 copy-start.2
  190.3 2.1 copy-start.4
  191.1 1.3 copy-start.1
  200.6 2.2 copy-start.2
  202.8 2.1 copy-start.4
  203.6 1.3 copy-start.1
Sparse Core Ops, SparseCore 0:
  87.7 30.3 all-gather.2
  214.0 41.2 reduce-scatter.1
